TPU v7x, 32 devices: a whole 2x2x4 slice. The times are simulated.
32 devices in a mesh: pipe: 4 (over x, core), expert: 4 (over z), tensor: 2 (over y).
Axes of the slice: x: 2, y: 2, z: 4, core: 2. Of those that a mesh axis runs over, the one named last changes fastest.
Arguments:
- stream: bfloat16 [2, 4, 64, 7168], P(None, 'pipe', 'expert', 'tensor'), may hold values from -6 to 6
- expert_ids: int32 [2, 4, 64, 2], P(None, 'pipe', 'expert'), may hold values from 0 to 3, all different within a row; in each aligned block of 16 rows (0 to 15, 16 to 31, ..., all dimensions but the last counted through in order) at most 12 rows name the same one
- norm_gain: float32 [4, 7168], P('pipe', 'tensor'), may hold values from 0.1 to 1.9
- router: float32 [4, 7168, 4], P('pipe', 'tensor'), may hold values from -0.0625 to 0.0625
- w_up: bfloat16 [4, 7168, 1024], P('expert', 'tensor'), may hold values from -0.0625 to 0.0625
- w_down: bfloat16 [4, 1024, 7168], P('expert', None, 'tensor'), may hold values from -0.1875 to 0.1875
Outputs:
- result: bfloat16 [2, 4, 64, 7168], P(None, 'pipe', 'expert', 'tensor')
Inputs may be any that keep to these rules, and one draw needn't show every extreme that they name: `expert_ids`: each token names 2 different experts. Among the 16 tokens of one direction held by one index of the expert axis at one section, at most 12 name any one expert, and in every draw some expert is named by exactly 12 of them.
All inputs are finite; a program needn't handle non-finite values.
Results may differ from a plain program's by a relative error of at most 0.0065.
Values may be sent and summed in bfloat16 or wider, within the bound.
A program may use at most 64 MiB of HBM per device.

v0:
```python
import jax
import jax.numpy as jnp
from jax import lax
from jax.sharding import PartitionSpec as P

norm_eps = 1e-06
route_scale = 2.5


def shifted(x, axis, by):
    size = lax.axis_size(axis)
    return lax.ppermute(x, axis, [(i, (i + by) % size) for i in range(size)])


def shards(stream, expert_ids, norm_gain, router, w_up, w_down):
    ahead = shifted(stream[0], "pipe", 1)
    behind = shifted(stream[1], "pipe", -1)
    arrived = jnp.concatenate([ahead, behind], axis=0).astype(jnp.float32)
    tok_rows = arrived.shape[1]
    quarter = arrived.shape[2]
    width = float(quarter * lax.axis_size("tensor"))
    scaled = arrived * norm_gain[0]
    squares = jnp.sum(arrived * arrived, axis=-1)
    highest = lax.Precision.HIGHEST
    total_sq = lax.psum(squares, "tensor")
    inverse = lax.rsqrt(total_sq / width + norm_eps)
    normed = scaled * inverse[..., None]
    logits = lax.psum(jnp.einsum("dtc,ce->dte", normed, router[0], precision=highest), "tensor")
    chosen = expert_ids[:, 0]
    fanout = chosen.shape[2]
    experts = router.shape[2]
    capacity = 3 * tok_rows * fanout // (2 * experts)
    picked = jnp.take_along_axis(logits, chosen, axis=-1)
    scores = jax.nn.sigmoid(picked)
    gates = route_scale * scores / jnp.sum(scores, axis=-1, keepdims=True)
    onehot = (chosen[..., None] == jnp.arange(experts, dtype=jnp.int32)).astype(jnp.int32)
    onehot = onehot.reshape(2, tok_rows * fanout, experts)
    earlier = jnp.cumsum(onehot, axis=1) - onehot
    within = jnp.sum(earlier * onehot, axis=-1).reshape(chosen.shape)
    heading = lax.broadcasted_iota(jnp.int32, chosen.shape, 0)
    member = lax.broadcasted_iota(jnp.int32, chosen.shape, 1)
    target = chosen * (2 * capacity) + heading * capacity + within
    anchor = heading * tok_rows + member
    owner = (
        jnp.full((experts * 2 * capacity,), 2 * tok_rows, jnp.int32)
        .at[target.reshape(-1)]
        .set(anchor.reshape(-1))
    )
    hidden = normed.astype(jnp.bfloat16).reshape(2 * tok_rows, quarter)
    table = jnp.concatenate([hidden, jnp.zeros((1, quarter), jnp.bfloat16)], axis=0)
    outgoing = table[owner].reshape(experts, 2 * capacity, quarter)
    upper = w_up[0]
    lower = w_down[0]
    received = lax.all_to_all(outgoing, "expert", split_axis=0, concat_axis=0, tiled=True)
    senders = received.shape[0]
    count = received.shape[1]
    inner = jnp.dot(received.reshape(-1, quarter), upper, preferred_element_type=jnp.float32)
    share = lax.psum_scatter(inner, "tensor", scatter_dimension=1, tiled=True)
    active = lax.all_gather(jax.nn.silu(share).astype(jnp.bfloat16), "tensor", axis=1, tiled=True)
    produced = jnp.dot(active, lower, preferred_element_type=jnp.float32).astype(jnp.bfloat16)
    answers = lax.all_to_all(
        produced.reshape(senders, count, quarter), "expert", split_axis=0, concat_axis=0, tiled=True
    )
    flat_back = answers.reshape(experts * 2 * capacity, quarter)
    gathered = (
        flat_back[target.reshape(-1)].reshape(2, tok_rows, fanout, quarter).astype(jnp.float32)
    )
    mixed = jnp.einsum("dtk,dtkc->dtc", gates, gathered)
    result = (arrived + mixed).astype(jnp.bfloat16)
    return result[:, None]


def solution(mesh):
    return jax.shard_map(
        shards,
        mesh=mesh,
        in_specs=(
            P(None, "pipe", "expert", "tensor"),
            P(None, "pipe", "expert", None),
            P("pipe", "tensor"),
            P("pipe", "tensor", None),
            P("expert", "tensor", None),
            P("expert", None, "tensor"),
        ),
        out_specs=P(None, "pipe", "expert", "tensor"),
        check_vma=False,
    )
```

profile of v0, /device:TPU:0, one launch (start us, length us, event | category | flops | bytes accessed | tf_op | source)
XLA Modules:
  0.0 101.9 jit_solution(15306226972587400173)
XLA Ops:
  6.5 1.0 slice_bitcast_fusion.1
  7.5 0.5 collective-permute-start
  8.1 2.0 %collective-permute-start.1 = (bf16[1,16,3584]{2,1,0:T(8,128)(2,1)S(1)}, bf16[1,16,3584]{2,1,0:T(8,128)(2,1)S(1)}, u32[]{:S(2)}, u32[]{:S(2)}) collective-permute-start(bf16[1,16,3584]{2,1,0:T(8,128)(2,1)S(1)} %get-tuple-element.8), channel_id=1, source_target_pairs={{0,24},{8,0},{16,8},{24,16},{1,25},{9,1},{17,9},{25,17},{2,26},{10... | collective-permute-start | bytes 344072 | tf_op jit(solution)/shard_map/ppermute | solution.py:12
  10.0 0.8 copy.14
  10.8 0.7 broadcast_multiply_fusion
  11.7 0.2 select_reduce_fusion
  12.1 0.1 mul.92
  12.3 0.1 iota.25
  12.5 0.1 reshape.149
  12.6 0.8 scatter_custom_fusion
  13.4 0.8 reduce
  14.2 0.1 multiply_reduce_fusion
  14.3 5.2 %psum.14 = f32[2,16]{1,0:T(2,128)S(1)} all-reduce(f32[2,16]{1,0:T(2,128)S(1)} %multiply_reduce_fusion), channel_id=1, replica_groups=mesh['pipe'=4,'expert'=4,'tensor'=2] {'tensor'}, use_global_device_ids=true, to_apply=%region_1.0 | all-reduce | flops 32 | bytes 256 | tf_op jit(solution)/shard_map/psum | solution.py:25
  19.6 0.1 fusion.9
  19.7 1.0 gather_fusion
  20.7 22.2 %all_to_all.10 = bf16[4,24,3584]{2,1,0:T(8,128)(2,1)S(1)} all-to-all(bf16[4,24,3584]{2,1,0:T(8,128)(2,1)S(1)} %bitcast.63), channel_id=1, replica_groups=mesh['pipe'=4,'expert'=4,'tensor'=2] {'expert'}, dimensions={0} | all-to-all | bytes 1376256 | tf_op jit(solution)/shard_map/all_to_all | solution.py:54
  42.8 5.1 %fusion.2 = f32[96,1024]{1,0:T(8,128)} fusion(bf16[96,3584]{1,0:T(8,128)(2,1)S(1)} %bitcast.62, bf16[1,3584,1024]{2,1,0:T(8,128)(2,1)} %param.10), kind=kOutput, calls=%fused_computation.6 | convolution fusion | flops 704643072 | bytes 8421376 | tf_op jit(solution)/shard_map/dot_general | solution.py:57
  48.0 11.9 %reduce-scatter.2.cloned.1.call-done = f32[96,512]{1,0:T(8,128)} async-done(((f32[96,1024]{1,0:T(8,128)}), f32[96,512]{1,0:T(8,128)}) %reduce-scatter.2.cloned.1.call-update) | async-done | bytes 196624 | tf_op jit(solution)/shard_map/reduce_scatter | solution.py:58
  59.9 1.0 multiply_convert_fusion
  60.9 5.3 %all_gather.3 = bf16[96,1024]{1,0:T(8,128)(2,1)S(1)} all-gather(bf16[96,512]{1,0:T(8,128)(2,1)S(1)} %multiply_convert_fusion), channel_id=1, replica_groups=mesh['pipe'=4,'expert'=4,'tensor'=2] {'tensor'}, dimensions={1}, use_global_device_ids=true | all-gather | bytes 294912 | tf_op jit(solution)/shard_map/all_gather | solution.py:59
  66.2 5.2 %fusion.4 = bf16[96,3584]{1,0:T(8,128)(2,1)} fusion(bf16[96,1024]{1,0:T(8,128)(2,1)S(1)} %all_gather.3, bf16[1,1024,3584]{2,1,0:T(8,128)(2,1)} %param.11), kind=kOutput, calls=%fused_computation.8 | convolution fusion | flops 704987136 | bytes 8224768 | tf_op jit(solution)/shard_map/dot_general | solution.py:60
  71.4 4.6 %all-to-all-start.1 = ((bf16[4,24,3584]{2,1,0:T(8,128)(2,1)}), bf16[4,24,3584]{2,1,0:T(8,128)(2,1)S(1)}, u32[]{:S(2)}, u32[]{:S(2)}) async-start(bf16[4,24,3584]{2,1,0:T(8,128)(2,1)} %bitcast.13), calls=%async_computation.2 | async-start | bytes 1376256 | tf_op jit(solution)/shard_map/all_to_all | solution.py:61
  76.1 0.1 reshape.139
  76.2 1.8 %fusion.10 = f32[2,16,4]{1,2,0:T(4,128)S(1)} fusion(f32[2,16]{1,0:T(2,128)S(1)} %add_rsqrt_fusion, f32[3584]{0:T(1024)S(1)} %reduce, f32[1,3584,4]{1,2,0:T(4,128)S(1)} %copy-done, bf16[1,16,3584]{2,1,0:T(8,128)(2,1)S(1)} %collective-permute-done.1, bf16[1,16,3584]{2,1,0:T(8,128)(2,1)S(1)} %collective-permute-done), kind=kOutput, calls=%fused_computation.14 | convolution fusion | flops 5963776 | bytes 301696 | tf_op jit(solution)/shard_map/dtc,ce->dte/dot_general | solution.py:28
  78.0 4.9 %psum.15 = f32[2,16,4]{1,2,0:T(4,128)S(1)} all-reduce(f32[2,16,4]{1,2,0:T(4,128)S(1)} %fusion.10), channel_id=1, replica_groups=mesh['pipe'=4,'expert'=4,'tensor'=2] {'tensor'}, use_global_device_ids=true, to_apply=%region_2.0 | all-reduce | flops 128 | bytes 1024 | tf_op jit(solution)/shard_map/psum | solution.py:28
  82.9 1.0 gather_fusion.2
  84.2 0.1 copy.15
  84.3 8.4 %all-to-all-done.1 = bf16[4,24,3584]{2,1,0:T(8,128)(2,1)S(1)} async-done(((bf16[4,24,3584]{2,1,0:T(8,128)(2,1)}), bf16[4,24,3584]{2,1,0:T(8,128)(2,1)S(1)}, u32[]{:S(2)}, u32[]{:S(2)}) %all-to-all-start.1) | async-done | bytes 688160 | tf_op jit(solution)/shard_map/all_to_all | solution.py:61
  92.7 0.8 gather_fusion.1
  93.5 0.2 reshape.121
  93.7 0.6 fusion.27
  94.3 0.7 fusion.14
  (30 shorter events, 1.0 us)
Async XLA Ops:
  6.5 69.7 %copy-start = (f32[1,3584,4]{1,2,0:T(4,128)S(1)}, f32[1,3584,4]{1,2,0:T(4,128)}, u32[]{:S(2)}) copy-start(f32[1,3584,4]{1,2,0:T(4,128)} %param.9) | copy-start | bytes 172036
  6.5 53.3 %reduce-scatter.2.cloned.1.call-start = ((), (), s32[]{:S(2)}) async-start(), calls=%async_computation.3 | async-start | bytes 589824 | tf_op jit(solution)/shard_map/reduce_scatter | solution.py:58
  7.5 6.6 %collective-permute-start = (bf16[1,16,3584]{2,1,0:T(8,128)(2,1)S(1)}, bf16[1,16,3584]{2,1,0:T(8,128)(2,1)S(1)}, u32[]{:S(2)}, u32[]{:S(2)}) collective-permute-start(bf16[1,16,3584]{2,1,0:T(8,128)(2,1)S(1)} %get-tuple-element.7), channel_id=1, source_target_pairs={{0,8},{8,16},{16,24},{24,0},{1,9},{9,17},{17,25},{25,1},{2,10},{10... | collective-permute-start | bytes 344072 | tf_op jit(solution)/shard_map/ppermute | solution.py:12
  8.1 6.1 %collective-permute-start.1 = (bf16[1,16,3584]{2,1,0:T(8,128)(2,1)S(1)}, bf16[1,16,3584]{2,1,0:T(8,128)(2,1)S(1)}, u32[]{:S(2)}, u32[]{:S(2)}) collective-permute-start(bf16[1,16,3584]{2,1,0:T(8,128)(2,1)S(1)} %get-tuple-element.8), channel_id=1, source_target_pairs={{0,24},{8,0},{16,8},{24,16},{1,25},{9,1},{17,9},{25,17},{2,26},{10... | collective-permute-start | bytes 344072 | tf_op jit(solution)/shard_map/ppermute | solution.py:12
  66.1 9.9 %copy-start.1 = (s32[2,1,16,2]{2,3,1,0:T(2,128)S(1)}, s32[2,1,16,2]{2,3,1,0:T(2,128)}, u32[]{:S(2)}) copy-start(s32[2,1,16,2]{2,3,1,0:T(2,128)} %param.7) | copy-start | bytes 772
  71.4 21.3 %all-to-all-start.1 = ((bf16[4,24,3584]{2,1,0:T(8,128)(2,1)}), bf16[4,24,3584]{2,1,0:T(8,128)(2,1)S(1)}, u32[]{:S(2)}, u32[]{:S(2)}) async-start(bf16[4,24,3584]{2,1,0:T(8,128)(2,1)} %bitcast.13), calls=%async_computation.2 | async-start | bytes 1376256 | tf_op jit(solution)/shard_map/all_to_all | solution.py:61
Sparse Core Ops, SparseCore 0:
  48.1 11.7 reduce-scatter.1
where the time goes:
time: 102 us
  blocking collectives  37.5 us (37%)
  waiting for transfers between devices  20.4 us (20%)
  between operations  13.6 us (13%)
  matrix products  12.8 us (13%)
  starting transfers between devices  7.13 us (7%)
  local copies, waits for them, and re-layouts  6.7 us (7%)
  other arithmetic  3.87 us (4%)
    all_to_all x1, blocking collectives, shards(): lax.all_to_all(outgoing, 'expert', split_axis=0, concat_axis=0, tiled=True)  22.2 us
    reduce_scatter x1, waiting for transfers between devices, shards(): share = lax.psum_scatter(inner, 'tensor', scatter_dimension=1, tiled=True)  11.9 us
    all_to_all x1, waiting for transfers between devices, shards(): lax.all_to_all(produced.reshape(senders, count, quarter), 'expert', split...  8.42 us
    all_gather x1, blocking collectives, shards(): lax.all_gather(jax.nn.silu(share).astype(jnp.bfloat16), 'tensor', axis=1,...  5.29 us
    dot_general x1, matrix products, shards(): jnp.dot(active, lower, preferred_element_type=jnp.float32)  5.25 us
    psum x1, blocking collectives, shards(): total_sq = lax.psum(squares, 'tensor')  5.16 us
    dot_general x1, matrix products, shards(): jnp.dot(received.reshape(-1, quarter), upper, preferred_element_type=jnp....  5.11 us
    psum x1, blocking collectives, shards(): lax.psum(jnp.einsum('dtc,ce->dte', normed, router[0], precision=highest),...  4.93 us
  transfers between devices with their start and end apart: 4, of which 2 were waited for; matrix products, arithmetic and copies ran while one was open for 7% of the time, Pallas kernels for 0%

commit v1 on v0

--- a/solution.py
+++ b/solution.py
@@ -5,6 +5,30 @@
 
 norm_eps = 1e-06
 route_scale = 2.5
+
+
+def in_blocks(x, dim, size):
+    shape = x.shape
+    blocks = x.reshape(*shape[:dim], size, shape[dim] // size, *shape[dim + 1 :])
+    return jnp.moveaxis(blocks, dim, 0)
+
+
+def laid_out(tiles, dim):
+    tiles = jnp.moveaxis(tiles, 0, dim)
+    lengths = tiles.shape
+    return tiles.reshape(*lengths[:dim], lengths[dim] * lengths[dim + 1], *lengths[dim + 2 :])
+
+
+def rotated_exchange(shard, axis, split_dim, concat_dim):
+    peers, index = (lax.axis_size(axis), lax.axis_index(axis))
+    blocks = in_blocks(shard, split_dim, peers)
+    result = blocks
+    for lap in range(1, peers):
+        target, source = ((index + lap) % peers, (index - lap) % peers)
+        sent = lax.dynamic_index_in_dim(blocks, target, 0)
+        received = lax.ppermute(sent, axis, [(i, (i + lap) % peers) for i in range(peers)])
+        result = lax.dynamic_update_slice_in_dim(result, received, source, axis=0)
+    return laid_out(result, concat_dim)
 
 
 def shifted(x, axis, by):
@@ -58,9 +82,7 @@
     share = lax.psum_scatter(inner, "tensor", scatter_dimension=1, tiled=True)
     active = lax.all_gather(jax.nn.silu(share).astype(jnp.bfloat16), "tensor", axis=1, tiled=True)
     produced = jnp.dot(active, lower, preferred_element_type=jnp.float32).astype(jnp.bfloat16)
-    answers = lax.all_to_all(
-        produced.reshape(senders, count, quarter), "expert", split_axis=0, concat_axis=0, tiled=True
-    )
+    answers = rotated_exchange(produced.reshape(senders, count, quarter), "expert", 0, 0)
     flat_back = answers.reshape(experts * 2 * capacity, quarter)
     gathered = (
         flat_back[target.reshape(-1)].reshape(2, tok_rows, fanout, quarter).astype(jnp.float32)

time: 102 us -> 97.3 us (0.954)
  waiting for transfers between devices: 20.4 us -> 17.3 us
    ppermute x0 -> x3, waiting for transfers between devices: none -> 12.7 us  [rotated_exchange(): lax.ppermute(sent, axis, [(i, (i + lap) % peers) for i in range(peers)])]
    all_to_all x1 -> x0, waiting for transfers between devices: 8.42 us -> none  [shards(): lax.all_to_all(produced.reshape(senders, count, quarter), 'expert', split...]
    reduce_scatter x1, waiting for transfers between devices: 11.9 us -> 4.16 us  [shards(): share = lax.psum_scatter(inner, 'tensor', scatter_dimension=1, tiled=True)]
    all_to_all x1 -> x0, starting transfers between devices: 4.6 us -> none  [shards(): lax.all_to_all(produced.reshape(senders, count, quarter), 'expert', split...]
    ppermute x0 -> x3, starting transfers between devices: none -> 3.7 us  [rotated_exchange(): lax.ppermute(sent, axis, [(i, (i + lap) % peers) for i in range(peers)])]
  transfers between devices with their start and end apart: 4 -> 6, of which waited for: 2 -> 4; matrix products, arithmetic and copies ran while one was open for 7% -> 8% of each run, Pallas kernels for 0% -> 0%
where the time goes in v1:
time: 97.3 us; the launch traced here: 96.9 us
  blocking collectives  37.1 us (38%)
  waiting for transfers between devices  17.3 us (18%)
  between operations  13.7 us (14%)
  matrix products  11.9 us (12%)
  local copies, waits for them, and re-layouts  6.82 us (7%)
  starting transfers between devices  6.16 us (6%)
  other arithmetic  3.86 us (4%)
    all_to_all x1, blocking collectives, shards(): lax.all_to_all(outgoing, 'expert', split_axis=0, concat_axis=0, tiled=True)  22 us
    ppermute x3, waiting for transfers between devices, rotated_exchange(): lax.ppermute(sent, axis, [(i, (i + lap) % peers) for i in range(peers)])  12.7 us
    all_gather x1, blocking collectives, shards(): lax.all_gather(jax.nn.silu(share).astype(jnp.bfloat16), 'tensor', axis=1,...  5.29 us
    dot_general x1, matrix products, shards(): jnp.dot(received.reshape(-1, quarter), upper, preferred_element_type=jnp....  5.13 us
    psum x1, blocking collectives, shards(): lax.psum(jnp.einsum('dtc,ce->dte', normed, router[0], precision=highest),...  4.93 us
    psum x1, blocking collectives, shards(): total_sq = lax.psum(squares, 'tensor')  4.92 us
    dot_general x1, matrix products, shards(): jnp.dot(active, lower, preferred_element_type=jnp.float32)  4.38 us
    reduce_scatter x1, waiting for transfers between devices, shards(): share = lax.psum_scatter(inner, 'tensor', scatter_dimension=1, tiled=True)  4.16 us
  transfers between devices with their start and end apart: 6, of which 4 were waited for; matrix products, arithmetic and copies ran while one was open for 8% of the time, Pallas kernels for 0%

profile of v1, /device:TPU:0, one launch (start us, length us, event | category | flops | bytes accessed | tf_op | source)
XLA Modules:
  0.0 96.9 jit_solution(13546419438020987189)
XLA Ops:
  6.5 1.0 %slice_bitcast_fusion.1 = (bf16[1,16,3584]{2,1,0:T(8,128)(2,1)S(1)}, bf16[1,16,3584]{2,1,0:T(8,128)(2,1)S(1)}) fusion(bf16[2,1,16,3584]{3,2,1,0:T(8,128)(2,1)} %param.6), kind=kLoop, calls=%fused_computation.25 | loop fusion | bytes 458752 | tf_op jit(solution)/shard_map/squeeze | solution.py:40
  7.5 2.5 %collective-permute-start.1 = (bf16[1,16,3584]{2,1,0:T(8,128)(2,1)S(1)}, bf16[1,16,3584]{2,1,0:T(8,128)(2,1)S(1)}, u32[]{:S(2)}, u32[]{:S(2)}) collective-permute-start(bf16[1,16,3584]{2,1,0:T(8,128)(2,1)S(1)} %get-tuple-element.11), channel_id=1, source_target_pairs={{0,24},{8,0},{16,8},{24,16},{1,25},{9,1},{17,9},{25,17},{2,26},{10... | collective-permute-start | bytes 344072 | tf_op jit(solution)/shard_map/ppermute | solution.py:36
  10.0 0.8 copy.14
  10.8 0.7 broadcast_multiply_fusion
  11.7 0.2 select_reduce_fusion
  12.0 0.1 mul.92
  12.2 0.1 iota.25
  12.4 0.1 reshape.141
  12.5 0.8 scatter_custom_fusion
  13.3 0.8 reduce
  14.1 0.5 collective-permute-done
  14.5 0.1 multiply_reduce_fusion
  14.7 4.9 %psum.14 = f32[2,16]{1,0:T(2,128)S(1)} all-reduce(f32[2,16]{1,0:T(2,128)S(1)} %multiply_reduce_fusion), channel_id=1, replica_groups=mesh['pipe'=4,'expert'=4,'tensor'=2] {'tensor'}, use_global_device_ids=true, to_apply=%region_1.0 | all-reduce | flops 32 | bytes 256 | tf_op jit(solution)/shard_map/psum | solution.py:49
  19.8 1.0 %gather_fusion = bf16[96,3584]{1,0:T(8,128)(2,1)S(1)} fusion(bf16[33,3584]{1,0:T(8,128)(2,1)S(1)} %concatenate.7, s32[1024]{0:T(1024)S(1)} %pad_clamp_fusion.1), kind=kCustom, calls=%fused_computation | custom fusion | bytes 1376640 | tf_op jit(solution)/shard_map/gather | solution.py:75
  20.8 22.0 %all_to_all.5 = bf16[4,24,3584]{2,1,0:T(8,128)(2,1)S(1)} all-to-all(bf16[4,24,3584]{2,1,0:T(8,128)(2,1)S(1)} %bitcast.65), channel_id=1, replica_groups=mesh['pipe'=4,'expert'=4,'tensor'=2] {'expert'}, dimensions={0} | all-to-all | bytes 1376256 | tf_op jit(solution)/shard_map/all_to_all | solution.py:78
  42.8 5.1 %fusion.2 = f32[96,1024]{1,0:T(8,128)} fusion(bf16[96,3584]{1,0:T(8,128)(2,1)S(1)} %bitcast.64, bf16[1,3584,1024]{2,1,0:T(8,128)(2,1)} %param.10), kind=kOutput, calls=%fused_computation.6 | convolution fusion | flops 704643072 | bytes 8421376 | tf_op jit(solution)/shard_map/dot_general | solution.py:81
  48.3 1.8 %fusion.10 = f32[2,16,4]{1,2,0:T(4,128)S(1)} fusion(f32[2,16]{1,0:T(2,128)S(1)} %add_rsqrt_fusion, f32[3584]{0:T(1024)S(1)} %reduce, f32[1,3584,4]{1,2,0:T(4,128)S(1)} %copy-done, bf16[1,16,3584]{2,1,0:T(8,128)(2,1)S(1)} %collective-permute-done.1, bf16[1,16,3584]{2,1,0:T(8,128)(2,1)S(1)} %collective-permute-done), kind=kOutput, calls=%fused_computation.14 | convolution fusion | flops 5963776 | bytes 301696 | tf_op jit(solution)/shard_map/dtc,ce->dte/dot_general | solution.py:52
  50.1 4.9 %psum.15 = f32[2,16,4]{1,2,0:T(4,128)S(1)} all-reduce(f32[2,16,4]{1,2,0:T(4,128)S(1)} %fusion.10), channel_id=1, replica_groups=mesh['pipe'=4,'expert'=4,'tensor'=2] {'tensor'}, use_global_device_ids=true, to_apply=%region_2.0 | all-reduce | flops 128 | bytes 1024 | tf_op jit(solution)/shard_map/psum | solution.py:52
  55.0 1.0 gather_fusion.2
  56.2 4.2 %reduce-scatter.2.cloned.1.call-done = f32[96,512]{1,0:T(8,128)} async-done(((f32[96,1024]{1,0:T(8,128)}), f32[96,512]{1,0:T(8,128)}) %reduce-scatter.2.cloned.1.call-update) | async-done | bytes 196624 | tf_op jit(solution)/shard_map/reduce_scatter | solution.py:82
  60.3 1.0 %multiply_convert_fusion = bf16[96,512]{1,0:T(8,128)(2,1)S(1)} fusion(f32[96,512]{1,0:T(8,128)} %reduce-scatter.2.cloned.1.call-done), kind=kLoop, calls=%fused_computation.23 | loop fusion | flops 245760 | bytes 294912 | tf_op jit(solution)/shard_map/convert_element_type | solution.py:83
  61.3 5.3 %all_gather.3 = bf16[96,1024]{1,0:T(8,128)(2,1)S(1)} all-gather(bf16[96,512]{1,0:T(8,128)(2,1)S(1)} %multiply_convert_fusion), channel_id=1, replica_groups=mesh['pipe'=4,'expert'=4,'tensor'=2] {'tensor'}, dimensions={1}, use_global_device_ids=true | all-gather | bytes 294912 | tf_op jit(solution)/shard_map/all_gather | solution.py:83
  66.6 4.4 %fusion.4 = bf16[96,3584]{1,0:T(8,128)(2,1)S(1)} fusion(bf16[96,1024]{1,0:T(8,128)(2,1)S(1)} %all_gather.3, bf16[1,1024,3584]{2,1,0:T(8,128)(2,1)} %param.11), kind=kOutput, calls=%fused_computation.8 | convolution fusion | flops 704987136 | bytes 8224768 | tf_op jit(solution)/shard_map/dot_general | solution.py:84
  71.0 1.5 %collective-permute-start.2 = (bf16[1,1,24,3584]{3,2,0,1:T(8,128)(2,1)S(1)}, bf16[1,1,24,3584]{3,2,0,1:T(8,128)(2,1)S(1)}, u32[]{:S(2)}, u32[]{:S(2)}) collective-permute-start(bf16[1,1,24,3584]{3,2,0,1:T(8,128)(2,1)S(1)} %constant_dynamic-slice_fusion.2), channel_id=1, source_target_pairs={{0,2},{2,4},{4,6},{6,0},{1,3},{3,5},{5,7},{7,1},{8,10},{10,12},{12... | collective-permute-start | bytes 516104 | tf_op jit(solution)/shard_map/ppermute | solution.py:29
  72.6 5.7 %collective-permute-done.2 = bf16[1,1,24,3584]{3,2,0,1:T(8,128)(2,1)S(1)} collective-permute-done((bf16[1,1,24,3584]{3,2,0,1:T(8,128)(2,1)S(1)}, bf16[1,1,24,3584]{3,2,0,1:T(8,128)(2,1)S(1)}, u32[]{:S(2)}, u32[]{:S(2)}) %collective-permute-start.2) | collective-permute-done | bytes 172064 | tf_op jit(solution)/shard_map/ppermute | solution.py:29
  78.3 0.7 collective-permute-start.3
  79.1 1.5 %collective-permute-start.4 = (bf16[1,1,24,3584]{3,2,0,1:T(8,128)(2,1)S(1)}, bf16[1,1,24,3584]{3,2,0,1:T(8,128)(2,1)S(1)}, u32[]{:S(2)}, u32[]{:S(2)}) collective-permute-start(bf16[1,1,24,3584]{3,2,0,1:T(8,128)(2,1)S(1)} %get-tuple-element.7), channel_id=1, source_target_pairs={{0,6},{2,0},{4,2},{6,4},{1,7},{3,1},{5,3},{7,5},{8,14},{10,8},{12,... | collective-permute-start | bytes 516104 | tf_op jit(solution)/shard_map/ppermute | solution.py:29
  80.6 7.0 %collective-permute-done.3 = bf16[1,1,24,3584]{3,2,0,1:T(8,128)(2,1)S(1)} collective-permute-done((bf16[1,1,24,3584]{3,2,0,1:T(8,128)(2,1)S(1)}, bf16[1,1,24,3584]{3,2,0,1:T(8,128)(2,1)S(1)}, u32[]{:S(2)}, u32[]{:S(2)}) %collective-permute-start.3) | collective-permute-done | bytes 172064 | tf_op jit(solution)/shard_map/ppermute | solution.py:29
  87.7 0.8 gather_fusion.1
  88.5 0.2 reshape.113
  88.7 0.6 fusion.27
  89.3 0.7 fusion.14
  (38 shorter events, 1.5 us)
Async XLA Ops:
  6.5 41.8 %copy-start = (f32[1,3584,4]{1,2,0:T(4,128)S(1)}, f32[1,3584,4]{1,2,0:T(4,128)}, u32[]{:S(2)}) copy-start(f32[1,3584,4]{1,2,0:T(4,128)} %param.9) | copy-start | bytes 172036
  6.5 53.8 %reduce-scatter.2.cloned.1.call-start = ((), (), s32[]{:S(2)}) async-start(), calls=%async_computation.2 | async-start | bytes 589824 | tf_op jit(solution)/shard_map/reduce_scatter | solution.py:82
  7.5 6.6 %collective-permute-start.1 = (bf16[1,16,3584]{2,1,0:T(8,128)(2,1)S(1)}, bf16[1,16,3584]{2,1,0:T(8,128)(2,1)S(1)}, u32[]{:S(2)}, u32[]{:S(2)}) collective-permute-start(bf16[1,16,3584]{2,1,0:T(8,128)(2,1)S(1)} %get-tuple-element.11), channel_id=1, source_target_pairs={{0,24},{8,0},{16,8},{24,16},{1,25},{9,1},{17,9},{25,17},{2,26},{10... | collective-permute-start | bytes 344072 | tf_op jit(solution)/shard_map/ppermute | solution.py:36
  10.0 4.6 %collective-permute-start = (bf16[1,16,3584]{2,1,0:T(8,128)(2,1)S(1)}, bf16[1,16,3584]{2,1,0:T(8,128)(2,1)S(1)}, u32[]{:S(2)}, u32[]{:S(2)}) collective-permute-start(bf16[1,16,3584]{2,1,0:T(8,128)(2,1)S(1)} %get-tuple-element.10), channel_id=1, source_target_pairs={{0,8},{8,16},{16,24},{24,0},{1,9},{9,17},{17,25},{25,1},{2,10},{10... | collective-permute-start | bytes 344072 | tf_op jit(solution)/shard_map/ppermute | solution.py:36
  42.8 5.2 %copy-start.1 = (s32[2,1,16,2]{2,3,1,0:T(2,128)S(1)}, s32[2,1,16,2]{2,3,1,0:T(2,128)}, u32[]{:S(2)}) copy-start(s32[2,1,16,2]{2,3,1,0:T(2,128)} %param.7) | copy-start | bytes 772
  71.0 7.3 %collective-permute-start.2 = (bf16[1,1,24,3584]{3,2,0,1:T(8,128)(2,1)S(1)}, bf16[1,1,24,3584]{3,2,0,1:T(8,128)(2,1)S(1)}, u32[]{:S(2)}, u32[]{:S(2)}) collective-permute-start(bf16[1,1,24,3584]{3,2,0,1:T(8,128)(2,1)S(1)} %constant_dynamic-slice_fusion.2), channel_id=1, source_target_pairs={{0,2},{2,4},{4,6},{6,0},{1,3},{3,5},{5,7},{7,1},{8,10},{10,12},{12... | collective-permute-start | bytes 516104 | tf_op jit(solution)/shard_map/ppermute | solution.py:29
  78.3 9.3 %collective-permute-start.3 = (bf16[1,1,24,3584]{3,2,0,1:T(8,128)(2,1)S(1)}, bf16[1,1,24,3584]{3,2,0,1:T(8,128)(2,1)S(1)}, u32[]{:S(2)}, u32[]{:S(2)}) collective-permute-start(bf16[1,1,24,3584]{3,2,0,1:T(8,128)(2,1)S(1)} %get-tuple-element.8), channel_id=1, source_target_pairs={{0,4},{2,6},{4,0},{6,2},{1,5},{3,7},{5,1},{7,3},{8,12},{10,14},{12... | collective-permute-start | bytes 516104 | tf_op jit(solution)/shard_map/ppermute | solution.py:29
  79.1 8.5 %collective-permute-start.4 = (bf16[1,1,24,3584]{3,2,0,1:T(8,128)(2,1)S(1)}, bf16[1,1,24,3584]{3,2,0,1:T(8,128)(2,1)S(1)}, u32[]{:S(2)}, u32[]{:S(2)}) collective-permute-start(bf16[1,1,24,3584]{3,2,0,1:T(8,128)(2,1)S(1)} %get-tuple-element.7), channel_id=1, source_target_pairs={{0,6},{2,0},{4,2},{6,4},{1,7},{3,1},{5,3},{7,5},{8,14},{10,8},{12,... | collective-permute-start | bytes 516104 | tf_op jit(solution)/shard_map/ppermute | solution.py:29
Sparse Core Ops, SparseCore 0:
  48.1 12.2 reduce-scatter.1
